TPU v7x, 256 devices: a whole 4x4x8 slice. The times are simulated.
256 devices in a mesh: sector: 32 (over x, z_lo, core), layer: 8 (over y, z_hi).
Axes of the slice: x: 4, y: 4, z: 8 (z_hi: 2, z_lo: 4; z = z_hi * 4 + z_lo), core: 2. Of those that a mesh axis runs over, the one named last changes fastest.
Arguments:
- rotor_state: float32 [5, 8, 128, 16384], P(None, None, 'layer', 'sector'), may hold values from -1.5 to 4, as said below
- cavity_state: float32 [5, 4, 128, 16384], P(None, None, 'layer', 'sector'), may hold values from -1.5 to 4, as said below
- block_map: int32 [32], replicated, may hold values from 0 to 31, each once
- rotor_offset: int32 [1], replicated, may hold values from 0 to 511
Outputs:
- rotor_next: float32 [5, 8, 128, 16384], P(None, None, 'layer', 'sector')
- cavity_next: float32 [5, 4, 128, 16384], P(None, None, 'layer', 'sector')
Inputs may be any that keep to these rules, and one draw needn't show every extreme that they name: `rotor_state`: component 0 lies in 0.5 to 1.5, components 1 to 3 in -1.5 to 1.5, component 4 in 2 to 4. `cavity_state`: component 0 lies in 0.5 to 1.5, components 1 to 3 in -1.5 to 1.5, component 4 in 2 to 4. `block_map`: each of 0 to 31 once.
All inputs are finite; a program needn't handle non-finite values.
Results may differ from a plain program's by a relative error of at most 0.00002.
Values sent between devices are 32-bit elements; how exact they have to be, the bound alone decides.
A program may use at most 192 MiB of HBM per device.

v0:
```python
import jax
import jax.numpy as jnp
from jax import lax
from jax.sharding import PartitionSpec as P

DIFFUSION = 0.05
COURANT = 0.1


def with_halo(cells, sides, width, closed):
    for axis, dim in sides:
        count = lax.axis_size(axis)
        ends = count if closed else count - 1
        head = lax.slice_in_dim(cells, 0, width, axis=dim)
        tail = lax.slice_in_dim(cells, cells.shape[dim] - width, cells.shape[dim], axis=dim)
        cells = jnp.concatenate(
            [
                lax.ppermute(tail, axis, [(i, (i + 1) % count) for i in range(ends)]),
                cells,
                lax.ppermute(head, axis, [((i + 1) % count, i) for i in range(ends)]),
            ],
            axis=dim,
        )
    return cells


def shifted(value, axis, steps):
    count = lax.axis_size(axis)
    pairs = [(source, (source + steps) % count) for source in range(count)]
    return lax.ppermute(value, axis, pairs)


def viscosity(density, energy):
    return 0.5 * (energy / density) ** 0.7


def region_update(region, seam_ghost, seam_last):
    cycle_padded = with_halo(region, (("sector", 3),), 1, True)
    radial_padded = with_halo(region, (("layer", 2),), 1, False)
    layer_here = lax.axis_index("layer")
    layers = lax.axis_size("layer")
    radial_rows = region.shape[2]
    viscous = viscosity(region[0], region[4])
    ghost_viscous = viscosity(seam_ghost[0], seam_ghost[4])
    if seam_last:
        extended = jnp.concatenate([region, seam_ghost[:, None]], axis=1)
        extended_mu = jnp.concatenate([viscous, ghost_viscous[None]], axis=0)
    else:
        extended = jnp.concatenate([seam_ghost[:, None], region], axis=1)
        extended_mu = jnp.concatenate([ghost_viscous[None], viscous], axis=0)
    face_axial = (
        0.5
        * (extended_mu[None, 1:] + extended_mu[None, :-1])
        * (extended[:, 1:] - extended[:, :-1])
    )
    empty_plane = jnp.zeros_like(face_axial[:, :1])
    if seam_last:
        axial_sum = face_axial - jnp.concatenate([empty_plane, face_axial[:, :-1]], axis=1)
    else:
        axial_sum = jnp.concatenate([face_axial[:, 1:], empty_plane], axis=1) - face_axial
    radial_mu = viscosity(radial_padded[0], radial_padded[4])
    face_radial = (
        0.5
        * (radial_mu[None, :, 1:] + radial_mu[None, :, :-1])
        * (radial_padded[:, :, 1:] - radial_padded[:, :, :-1])
    )
    face_index = jnp.arange(radial_rows + 1, dtype=jnp.int32)
    closed = (face_index == 0) & (layer_here == 0) | (face_index == radial_rows) & (
        layer_here == layers - 1
    )
    face_radial = jnp.where(closed[None, None, :, None], 0.0, face_radial)
    radial = face_radial[:, :, 1:] - face_radial[:, :, :-1]
    cycle_mu = viscosity(cycle_padded[0], cycle_padded[4])
    face_cycle = (
        0.5
        * (cycle_mu[None, ..., 1:] + cycle_mu[None, ..., :-1])
        * (cycle_padded[..., 1:] - cycle_padded[..., :-1])
    )
    cycle_sum = face_cycle[..., 1:] - face_cycle[..., :-1]
    velocity = cycle_padded[3] / cycle_padded[0]
    carried = velocity[None] * cycle_padded
    advected = -COURANT * 0.5 * (carried[..., 2:] - carried[..., :-2])
    return region + DIFFUSION * (axial_sum + radial + cycle_sum) + advected


def shards(rotor_state, cavity_state, block_map, rotor_offset):
    sectors = lax.axis_size("sector")
    position = lax.axis_index("sector")
    components = rotor_state.shape[0]
    radial_rows = rotor_state.shape[2]
    cycle_cells = rotor_state.shape[3]
    block_cells = cycle_cells // sectors
    offset_cells = rotor_offset[0]
    slot_index = jnp.arange(sectors, dtype=jnp.int32)
    rotor_seam = rotor_state[:, -1].reshape(components, radial_rows, sectors, block_cells)
    cavity_seam = cavity_state[:, 0]
    following = shifted(cavity_seam, "sector", -1)
    lifted = lax.dynamic_slice_in_dim(
        jnp.concatenate([cavity_seam, following], axis=2), offset_cells, cycle_cells, axis=2
    )
    lifted = lifted.reshape(components, radial_rows, sectors, block_cells)
    every_rotor = lax.all_gather(rotor_seam, "sector", axis=2, tiled=True)
    landed = jnp.take(every_rotor, (position - block_map) % sectors * sectors + slot_index, axis=2)
    every_cavity = lax.all_gather(lifted, "sector", axis=2, tiled=True)
    returned = jnp.take(
        every_cavity, (position + block_map) % sectors * sectors + slot_index, axis=2
    )
    landed_flat = landed.reshape(components, radial_rows, cycle_cells)
    preceding = shifted(landed_flat, "sector", 1)
    cavity_ghost = lax.dynamic_slice_in_dim(
        jnp.concatenate([preceding, landed_flat], axis=2),
        cycle_cells - offset_cells,
        cycle_cells,
        axis=2,
    )
    rotor_ghost = returned.reshape(components, radial_rows, cycle_cells)
    rotor_next = region_update(rotor_state, rotor_ghost, True)
    cavity_next = region_update(cavity_state, cavity_ghost, False)
    return (rotor_next, cavity_next)


def solution(mesh):
    placed = (P(None, None, "layer", "sector"), P(None, None, "layer", "sector"), P(), P())
    return jax.shard_map(
        shards,
        mesh=mesh,
        in_specs=placed,
        out_specs=(P(None, None, "layer", "sector"), P(None, None, "layer", "sector")),
        check_vma=False,
    )
```

profile of v0, /device:TPU:1, one launch (start us, length us, event | category | flops | bytes accessed | tf_op | source)
XLA Modules:
  0.0 520.8 jit_solution(2654275196244347219)
XLA Ops:
  8.6 1.8 copy.22
  10.5 1.0 copy-done.1
  11.5 3.3 collective-permute-start
  15.4 2.2 collective-permute-done
  18.2 1.8 copy.12
  20.3 5.6 %collective-permute-start.9 = (f32[5,4,16,1]{3,2,1,0:T(8,128)S(1)}, f32[5,4,16,1]{3,2,1,0:T(8,128)S(1)}, u32[]{:S(2)}, u32[]{:S(2)}) collective-permute-start(f32[5,4,16,1]{3,2,1,0:T(8,128)S(1)} %get-tuple-element.18), channel_id=1, source_target_pairs={{8,0},{16,8},{24,16},{32,24},{40,32},{48,40},{56,48},{64,56},{72,6... | collective-permute-start | bytes 3848 | tf_op jit(solution)/shard_map/ppermute | solution.py:20
  26.6 5.1 collective-permute-start.6
  31.8 1.3 collective-permute-start.7
  37.2 6.1 %collective-permute-start.4 = (f32[5,8,16,1]{3,2,1,0:T(8,128)}, f32[5,8,16,1]{3,2,1,0:T(8,128)S(1)}, u32[]{:S(2)}, u32[]{:S(2)}) collective-permute-start(f32[5,8,16,1]{3,2,1,0:T(8,128)} %get-tuple-element.12), channel_id=1, source_target_pairs={{8,0},{16,8},{24,16},{32,24},{40,32},{48,40},{56,48},{64,56},{72,6... | collective-permute-start | bytes 7688 | tf_op jit(solution)/shard_map/ppermute | solution.py:20
  43.3 8.2 %collective-permute-start.1 = (f32[5,8,1,512]{3,1,2,0:T(8,128)}, f32[5,8,1,512]{3,1,2,0:T(8,128)S(1)}, u32[]{:S(2)}, u32[]{:S(2)}) collective-permute-start(f32[5,8,1,512]{3,1,2,0:T(8,128)} %copy.24), channel_id=1, source_target_pairs={{0,1},{1,2},{2,3},{3,4},{4,5},{5,6},{6,7},{8,9},{9,10},{10,11},{11... | collective-permute-start | bytes 245768 | tf_op jit(solution)/shard_map/ppermute | solution.py:18
  52.3 1.3 broadcast_multiply_fusion.1
  53.6 1.5 collective-permute-start.2
  56.3 1.7 fusion.2
  58.0 1.8 broadcast_multiply_fusion
  60.0 1.2 fusion.12
  61.3 4.0 collective-permute-done.2
  65.8 1.8 fusion.1
  67.6 187.4 %all-gather.5.cloned.1.call-done = f32[5,16,1024,16]{3,1,2,0:T(8,128)} async-done(((f32[5,16,32,16]{3,1,2,0:T(8,128)}), f32[5,16,1024,16]{3,1,2,0:T(8,128)}) %all-gather.5.cloned.1.call-update) | async-done | bytes 5242896 | tf_op jit(solution)/shard_map/all_gather | solution.py:102
  255.0 3.0 gather_fusion.1
  258.0 230.7 %all-gather.3.cloned.1.call-done = f32[5,16,1024,16]{3,1,2,0:T(8,128)} async-done(((f32[5,16,32,16]{3,1,2,0:T(8,128)}), f32[5,16,1024,16]{3,1,2,0:T(8,128)}) %all-gather.3.cloned.1.call-update) | async-done | bytes 5242896 | tf_op jit(solution)/shard_map/all_gather | solution.py:104
  488.7 3.0 gather_fusion
  491.8 1.9 select_bitcast_fusion
  493.7 1.5 copy.14
  495.4 1.5 copy.23
  496.8 2.8 reshape.106
  499.7 1.4 collective-permute-start.5
  501.1 2.1 broadcast_in_dim_reshape.3
  504.0 1.1 mul.216
  505.6 1.0 copy-done.3
  507.7 2.1 fusion.4
  509.9 1.1 fusion.41
  512.5 1.4 fusion.15
  (73 shorter events, 14.0 us)
Async XLA Ops:
  7.2 247.8 %all-gather.5.cloned.1.call-start = ((), (), s32[]{:S(2)}) async-start(), calls=%async_computation.1 | async-start | bytes 43253760 | tf_op jit(solution)/shard_map/all_gather | solution.py:102
  10.4 1.1 copy-start.1
  10.4 478.3 %all-gather.3.cloned.1.call-start = ((), (), s32[]{:S(2)}) async-start(), calls=%async_computation | async-start | bytes 43253760 | tf_op jit(solution)/shard_map/all_gather | solution.py:104
  11.5 6.1 %collective-permute-start = (f32[5,16,512]{2,1,0:T(8,128)S(1)}, f32[5,16,512]{2,1,0:T(8,128)S(1)}, u32[]{:S(2)}, u32[]{:S(2)}) collective-permute-start(f32[5,16,512]{2,1,0:T(8,128)S(1)} %slice_bitcast_fusion), channel_id=1, source_target_pairs={{0,248},{8,0},{16,8},{24,16},{32,24},{40,32},{48,40},{56,48},{64,5... | collective-permute-start | bytes 491528 | tf_op jit(solution)/shard_map/ppermute | solution.py:30
  20.1 13.0 %copy-start = (f32[5,8,16,512]{3,2,1,0:T(8,128)S(1)}, f32[5,8,16,512]{3,2,1,0:T(8,128)}, u32[]{:S(2)}) copy-start(f32[5,8,16,512]{3,2,1,0:T(8,128)} %param.6) | copy-start | bytes 3932164
  20.1 13.9 %copy-start.10 = (s32[32]{0:T(128)S(1)}, s32[32]{0:T(128)}, u32[]{:S(2)}) copy-start(s32[32]{0:T(128)} %param.8) | copy-start | bytes 388
  20.2 17.0 %collective-permute-start.8 = (f32[5,4,16,1]{3,2,1,0:T(8,128)S(1)}, f32[5,4,16,1]{3,2,1,0:T(8,128)S(1)}, u32[]{:S(2)}, u32[]{:S(2)}) collective-permute-start(f32[5,4,16,1]{3,2,1,0:T(8,128)S(1)} %get-tuple-element.17), channel_id=1, source_target_pairs={{0,8},{8,16},{16,24},{24,32},{32,40},{40,48},{48,56},{56,64},{64,7... | collective-permute-start | bytes 3848 | tf_op jit(solution)/shard_map/ppermute | solution.py:18
  20.3 23.0 %collective-permute-start.9 = (f32[5,4,16,1]{3,2,1,0:T(8,128)S(1)}, f32[5,4,16,1]{3,2,1,0:T(8,128)S(1)}, u32[]{:S(2)}, u32[]{:S(2)}) collective-permute-start(f32[5,4,16,1]{3,2,1,0:T(8,128)S(1)} %get-tuple-element.18), channel_id=1, source_target_pairs={{8,0},{16,8},{24,16},{32,24},{40,32},{48,40},{56,48},{64,56},{72,6... | collective-permute-start | bytes 3848 | tf_op jit(solution)/shard_map/ppermute | solution.py:20
  26.6 33.2 %collective-permute-start.6 = (f32[5,4,1,512]{3,2,1,0:T(1,128)}, f32[5,4,1,512]{3,2,1,0:T(1,128)S(1)}, u32[]{:S(2)}, u32[]{:S(2)}) collective-permute-start(f32[5,4,1,512]{3,2,1,0:T(1,128)} %get-tuple-element.15), channel_id=1, source_target_pairs={{0,1},{1,2},{2,3},{3,4},{4,5},{5,6},{6,7},{8,9},{9,10},{10,11},{11... | collective-permute-start | bytes 122888 | tf_op jit(solution)/shard_map/ppermute | solution.py:18
  31.8 28.1 %collective-permute-start.7 = (f32[5,4,1,512]{3,2,1,0:T(1,128)}, f32[5,4,1,512]{3,2,1,0:T(1,128)S(1)}, u32[]{:S(2)}, u32[]{:S(2)}) collective-permute-start(f32[5,4,1,512]{3,2,1,0:T(1,128)} %get-tuple-element.16), channel_id=1, source_target_pairs={{1,0},{2,1},{3,2},{4,3},{5,4},{6,5},{7,6},{9,8},{10,9},{11,10},{12... | collective-permute-start | bytes 122888 | tf_op jit(solution)/shard_map/ppermute | solution.py:20
  34.0 19.6 %collective-permute-start.3 = (f32[5,8,16,1]{3,2,1,0:T(8,128)}, f32[5,8,16,1]{3,2,1,0:T(8,128)S(1)}, u32[]{:S(2)}, u32[]{:S(2)}) collective-permute-start(f32[5,8,16,1]{3,2,1,0:T(8,128)} %get-tuple-element.11), channel_id=1, source_target_pairs={{0,8},{8,16},{16,24},{24,32},{32,40},{40,48},{48,56},{56,64},{64,7... | collective-permute-start | bytes 7688 | tf_op jit(solution)/shard_map/ppermute | solution.py:18
  37.2 18.2 %collective-permute-start.4 = (f32[5,8,16,1]{3,2,1,0:T(8,128)}, f32[5,8,16,1]{3,2,1,0:T(8,128)S(1)}, u32[]{:S(2)}, u32[]{:S(2)}) collective-permute-start(f32[5,8,16,1]{3,2,1,0:T(8,128)} %get-tuple-element.12), channel_id=1, source_target_pairs={{8,0},{16,8},{24,16},{32,24},{40,32},{48,40},{56,48},{64,56},{72,6... | collective-permute-start | bytes 7688 | tf_op jit(solution)/shard_map/ppermute | solution.py:20
  43.3 18.0 %collective-permute-start.1 = (f32[5,8,1,512]{3,1,2,0:T(8,128)}, f32[5,8,1,512]{3,1,2,0:T(8,128)S(1)}, u32[]{:S(2)}, u32[]{:S(2)}) collective-permute-start(f32[5,8,1,512]{3,1,2,0:T(8,128)} %copy.24), channel_id=1, source_target_pairs={{0,1},{1,2},{2,3},{3,4},{4,5},{5,6},{6,7},{8,9},{9,10},{10,11},{11... | collective-permute-start | bytes 245768 | tf_op jit(solution)/shard_map/ppermute | solution.py:18
  52.3 1.3 copy-start.9
  53.6 11.7 %collective-permute-start.2 = (f32[5,8,1,512]{3,1,2,0:T(8,128)S(1)}, f32[5,8,1,512]{3,1,2,0:T(8,128)S(1)}, u32[]{:S(2)}, u32[]{:S(2)}) collective-permute-start(f32[5,8,1,512]{3,1,2,0:T(8,128)S(1)} %copy-done.9), channel_id=1, source_target_pairs={{1,0},{2,1},{3,2},{4,3},{5,4},{6,5},{7,6},{9,8},{10,9},{11,10},{12... | collective-permute-start | bytes 245768 | tf_op jit(solution)/shard_map/ppermute | solution.py:20
  499.7 5.4 %copy-start.7 = (f32[8,16,512]{2,1,0:T(8,128)S(1)}, f32[8,16,512]{2,1,0:T(8,128)}, u32[]{:S(2)}) copy-start(f32[8,16,512]{2,1,0:T(8,128)} %multiply_bitcast_fusion) | copy-start | bytes 786436
  499.7 10.2 %collective-permute-start.5 = (f32[5,16,512]{2,1,0:T(8,128)}, f32[5,16,512]{2,1,0:T(8,128)}, u32[]{:S(2)}, u32[]{:S(2)}) collective-permute-start(f32[5,16,512]{2,1,0:T(8,128)} %reshape.106), channel_id=1, source_target_pairs={{0,8},{8,16},{16,24},{24,32},{32,40},{40,48},{48,56},{56,64},{64,7... | collective-permute-start | bytes 491528 | tf_op jit(solution)/shard_map/ppermute | solution.py:30
  505.1 1.4 copy-start.3
  505.1 2.0 copy-start.4
  505.4 2.3 copy-start.2
  507.7 3.3 copy-start.8
  511.0 1.1 copy-start.5
  511.0 1.4 copy-start.6
Sparse Core Ops, SparseCore 0:
  10.6 244.3 all-gather.4
  256.9 231.8 all-gather.2
where the time goes:
time: 521 us
  waiting for transfers between devices  425 us (82%)
  starting transfers between devices  32.6 us (6%)
  local copies, waits for them, and re-layouts  29.2 us (6%)
  other arithmetic  19.2 us (4%)
  between operations  15 us (3%)
    all_gather x1, waiting for transfers between devices, shards(): every_cavity = lax.all_gather(lifted, 'sector', axis=2, tiled=True)  231 us
    all_gather x1, waiting for transfers between devices, shards(): every_rotor = lax.all_gather(rotor_seam, 'sector', axis=2, tiled=True)  187 us
    ppermute x4, starting transfers between devices, with_halo(): lax.ppermute(head, axis, [((i + 1) % count, i) for i in range(ends)])  14.5 us
    ppermute x4, starting transfers between devices, with_halo(): lax.ppermute(tail, axis, [(i, (i + 1) % count) for i in range(ends)])  13.4 us
  transfers between devices with their start and end apart: 12, of which 5 were waited for; matrix products, arithmetic and copies ran while one was open for 5% of the time, Pallas kernels for 0%

commit v1 on v0

--- a/solution.py
+++ b/solution.py
@@ -101,7 +101,9 @@
     lifted = lifted.reshape(components, radial_rows, sectors, block_cells)
     every_rotor = lax.all_gather(rotor_seam, "sector", axis=2, tiled=True)
     landed = jnp.take(every_rotor, (position - block_map) % sectors * sectors + slot_index, axis=2)
-    every_cavity = lax.all_gather(lifted, "sector", axis=2, tiled=True)
+    every_cavity = jnp.concatenate(
+        lax.all_to_all(jnp.stack([lifted] * lax.axis_size("sector")), "sector", 0, 0), axis=2
+    )
     returned = jnp.take(
         every_cavity, (position + block_map) % sectors * sectors + slot_index, axis=2
     )

time: 521 us -> 498 us (0.956)
  waiting for transfers between devices: 425 us -> 275 us
  local copies, waits for them, and re-layouts: 29.2 us -> 124 us
  other arithmetic: 19.2 us -> 35.9 us
  starting transfers between devices: 32.6 us -> 43.9 us
    all_gather x1 -> x0, waiting for transfers between devices: 231 us -> none  [shards(): every_cavity = lax.all_gather(lifted, 'sector', axis=2, tiled=True)]
    ppermute x4, waiting for transfers between devices: 0.01 us -> 151 us  [with_halo(): lax.ppermute(tail, axis, [(i, (i + 1) % count) for i in range(ends)])]
    all_gather x1, waiting for transfers between devices: 187 us -> 112 us  [shards(): every_rotor = lax.all_gather(rotor_seam, 'sector', axis=2, tiled=True)]
    unnamed x24 -> x27, local copies, waits for them, and re-layouts: 5.74 us -> 54.4 us
    reshape x2, local copies, waits for them, and re-layouts: 2.27 us -> 46 us  [shards(): jnp.concatenate(lax.all_to_all(jnp.stack([lifted] * lax.axis_size('sector...]
    all_to_all x0 -> x1, other arithmetic: none -> 16.7 us  [shards(): lax.all_to_all(jnp.stack([lifted] * lax.axis_size('sector')), 'sector', 0...]
    ppermute x4, starting transfers between devices: 14.5 us -> 2.76 us  [with_halo(): lax.ppermute(head, axis, [((i + 1) % count, i) for i in range(ends)])]
    all_to_all x0 -> x1, starting transfers between devices: none -> 11.2 us  [shards(): lax.all_to_all(jnp.stack([lifted] * lax.axis_size('sector')), 'sector', 0...]
  transfers between devices with their start and end apart: 12 -> 12, of which waited for: 5 -> 3; matrix products, arithmetic and copies ran while one was open for 5% -> 12% of each run, Pallas kernels for 0% -> 0%
where the time goes in v1:
time: 498 us; the launch traced here: 494 us
  waiting for transfers between devices  275 us (55%)
  local copies, waits for them, and re-layouts  124 us (25%)
  starting transfers between devices  43.9 us (9%)
  other arithmetic  35.9 us (7%)
  between operations  15.1 us (3%)
    ppermute x4, waiting for transfers between devices, with_halo(): lax.ppermute(tail, axis, [(i, (i + 1) % count) for i in range(ends)])  151 us
    all_gather x1, waiting for transfers between devices, shards(): every_rotor = lax.all_gather(rotor_seam, 'sector', axis=2, tiled=True)  112 us
    unnamed x27, local copies, waits for them, and re-layouts  54.4 us
    reshape x2, local copies, waits for them, and re-layouts, shards(): jnp.concatenate(lax.all_to_all(jnp.stack([lifted] * lax.axis_size('sector...  46 us
    ppermute x4, starting transfers between devices, with_halo(): lax.ppermute(tail, axis, [(i, (i + 1) % count) for i in range(ends)])  17.1 us
    all_to_all x1, other arithmetic, shards(): lax.all_to_all(jnp.stack([lifted] * lax.axis_size('sector')), 'sector', 0...  16.7 us
    ppermute x2, starting transfers between devices, shifted(): return lax.ppermute(value, axis, pairs)  12.8 us
    ppermute x4, waiting for transfers between devices, with_halo(): lax.ppermute(head, axis, [((i + 1) % count, i) for i in range(ends)])  12.5 us
  transfers between devices with their start and end apart: 12, of which 3 were waited for; matrix products, arithmetic and copies ran while one was open for 12% of the time, Pallas kernels for 0%

profile of v1, /device:TPU:1, one launch (start us, length us, event | category | flops | bytes accessed | tf_op | source)
XLA Modules:
  0.0 493.8 jit_solution(11897845572943086959)
XLA Ops:
  8.1 3.3 collective-permute-start
  12.8 1.8 copy.25
  16.3 9.6 %broadcast_bitcast_fusion = f32[32,5,16,16,32]{4,3,2,1,0:T(8,128)} fusion(f32[5,16,32,16]{2,3,1,0:T(8,128)S(1)} %copy.13), kind=kLoop, calls=%fused_computation.119 | loop fusion | bytes 5406720
  25.9 18.7 %reshape.135 = f32[32,1,40960]{2,1,0:T(1,128)} reshape(f32[32,5,16,16,32]{4,3,2,1,0:T(8,128)} %broadcast_bitcast_fusion) | data formatting | bytes 10485760
  44.7 11.2 %all-to-all-start = ((f32[32,1,40960]{2,1,0:T(1,128)}), f32[32,1,40960]{2,1,0:T(1,128)}, u32[]{:S(2)}, u32[]{:S(2)}) async-start(f32[32,1,40960]{2,1,0:T(1,128)} %reshape.135), calls=%async_computation | async-start | bytes 10485760 | tf_op jit(solution)/shard_map/all_to_all | solution.py:105
  56.0 1.7 collective-permute-start.8
  58.4 6.2 %collective-permute-start.6 = (f32[5,4,1,512]{3,2,1,0:T(1,128)}, f32[5,4,1,512]{3,2,1,0:T(1,128)S(1)}, u32[]{:S(2)}, u32[]{:S(2)}) collective-permute-start(f32[5,4,1,512]{3,2,1,0:T(1,128)} %get-tuple-element.15), channel_id=1, source_target_pairs={{0,1},{1,2},{2,3},{3,4},{4,5},{5,6},{6,7},{8,9},{9,10},{10,11},{11... | collective-permute-start | bytes 122888 | tf_op jit(solution)/shard_map/ppermute | solution.py:18
  64.6 1.3 collective-permute-start.7
  66.9 2.0 collective-permute-start.3
  72.0 150.7 %collective-permute-done.8 = f32[5,4,16,1]{3,2,1,0:T(8,128)S(1)} collective-permute-done((f32[5,4,16,1]{3,2,1,0:T(8,128)S(1)}, f32[5,4,16,1]{3,2,1,0:T(8,128)S(1)}, u32[]{:S(2)}, u32[]{:S(2)}) %collective-permute-start.8) | collective-permute-done | bytes 1312 | tf_op jit(solution)/shard_map/ppermute | solution.py:18
  222.8 7.2 %collective-permute-start.1 = (f32[5,8,1,512]{3,1,2,0:T(8,128)}, f32[5,8,1,512]{3,1,2,0:T(8,128)S(1)}, u32[]{:S(2)}, u32[]{:S(2)}) collective-permute-start(f32[5,8,1,512]{3,1,2,0:T(8,128)} %copy.29), channel_id=1, source_target_pairs={{0,1},{1,2},{2,3},{3,4},{4,5},{5,6},{6,7},{8,9},{9,10},{10,11},{11... | collective-permute-start | bytes 245768 | tf_op jit(solution)/shard_map/ppermute | solution.py:18
  230.8 1.3 broadcast_multiply_fusion.1
  232.1 1.5 collective-permute-start.2
  233.6 12.4 %collective-permute-done.4 = f32[5,8,16,1]{3,2,1,0:T(8,128)S(1)} collective-permute-done((f32[5,8,16,1]{3,2,1,0:T(8,128)}, f32[5,8,16,1]{3,2,1,0:T(8,128)S(1)}, u32[]{:S(2)}, u32[]{:S(2)}) %collective-permute-start.4) | collective-permute-done | bytes 2592 | tf_op jit(solution)/shard_map/ppermute | solution.py:20
  247.0 1.7 fusion.2
  248.7 1.8 broadcast_multiply_fusion
  252.6 1.8 fusion.1
  254.3 111.9 %all-gather.2.cloned.1.call-done = f32[5,16,1024,16]{3,1,2,0:T(8,128)} async-done(((f32[5,16,32,16]{3,1,2,0:T(8,128)}), f32[5,16,1024,16]{3,1,2,0:T(8,128)}) %all-gather.2.cloned.1.call-update) | async-done | bytes 5242896 | tf_op jit(solution)/shard_map/all_gather | solution.py:102
  366.2 3.0 gather_fusion.1
  369.8 16.7 %reduce = f32[32,40960]{1,0:T(8,128)} reduce(f32[32,1,40960]{2,1,0:T(1,128)} %all-to-all-done, f32[]{:T(128)} %broadcast.148), dimensions={1}, to_apply=%all_to_all.3.reduce_sub_computation | reduce | bytes 10485764 | tf_op jit(solution)/shard_map/all_to_all | solution.py:105
  386.5 21.3 %reshape.136 = f32[32,5,16,16,32]{4,3,2,1,0:T(8,128)} reshape(f32[32,40960]{1,0:T(8,128)} %reduce) | data formatting | bytes 10485760
  407.7 16.1 %bitcast_bitcast_fusion = f32[5,16,32,32,16]{3,4,1,0,2:T(8,128)} fusion(f32[32,5,16,16,32]{4,3,2,1,0:T(8,128)} %reshape.136), kind=kLoop, calls=%fused_computation.118 | loop fusion | bytes 10485760 | tf_op jit(solution)/shard_map/reshape | solution.py:104
  423.8 30.0 %copy.27 = f32[5,16,32,32,16]{4,1,3,2,0:T(8,128)} copy(f32[5,16,32,32,16]{3,4,1,0,2:T(8,128)} %bitcast_bitcast_fusion) | data formatting | bytes 10485760 | tf_op jit(solution)/shard_map/reshape | solution.py:104
  453.8 3.0 gather_fusion
  456.8 1.9 select_bitcast_fusion
  458.8 1.5 copy.17
  460.4 1.5 copy.26
  461.9 2.8 reshape.112
  464.7 9.5 %collective-permute-start.5 = (f32[5,16,512]{2,1,0:T(8,128)}, f32[5,16,512]{2,1,0:T(8,128)}, u32[]{:S(2)}, u32[]{:S(2)}) collective-permute-start(f32[5,16,512]{2,1,0:T(8,128)} %reshape.112), channel_id=1, source_target_pairs={{0,8},{8,16},{16,24},{24,32},{32,40},{40,48},{48,56},{56,64},{64,7... | collective-permute-start | bytes 491528 | tf_op jit(solution)/shard_map/ppermute | solution.py:30
  474.2 2.1 broadcast_in_dim_reshape.3
  480.8 2.1 fusion.4
  485.6 1.4 fusion.15
  (79 shorter events, 19.7 us)
Async XLA Ops:
  7.2 359.1 %all-gather.2.cloned.1.call-start = ((), (), s32[]{:S(2)}) async-start(), calls=%async_computation.1 | async-start | bytes 43253760 | tf_op jit(solution)/shard_map/all_gather | solution.py:102
  8.1 7.2 %collective-permute-start = (f32[5,16,512]{2,1,0:T(8,128)S(1)}, f32[5,16,512]{2,1,0:T(8,128)S(1)}, u32[]{:S(2)}, u32[]{:S(2)}) collective-permute-start(f32[5,16,512]{2,1,0:T(8,128)S(1)} %slice_bitcast_fusion), channel_id=1, source_target_pairs={{0,248},{8,0},{16,8},{24,16},{32,24},{40,32},{48,40},{56,48},{64,5... | collective-permute-start | bytes 491528 | tf_op jit(solution)/shard_map/ppermute | solution.py:30
  44.7 11.2 %copy-start.1 = (f32[5,4,16,512]{3,2,1,0:T(8,128)S(1)}, f32[5,4,16,512]{3,2,1,0:T(8,128)}, u32[]{:S(2)}) copy-start(f32[5,4,16,512]{3,2,1,0:T(8,128)} %param.7) | copy-start | bytes 1966084
  44.7 21.3 %copy-start = (f32[5,8,16,512]{3,2,1,0:T(8,128)S(1)}, f32[5,8,16,512]{3,2,1,0:T(8,128)}, u32[]{:S(2)}) copy-start(f32[5,8,16,512]{3,2,1,0:T(8,128)} %param.6) | copy-start | bytes 3932164
  44.7 324.6 %all-to-all-start = ((f32[32,1,40960]{2,1,0:T(1,128)}), f32[32,1,40960]{2,1,0:T(1,128)}, u32[]{:S(2)}, u32[]{:S(2)}) async-start(f32[32,1,40960]{2,1,0:T(1,128)} %reshape.135), calls=%async_computation | async-start | bytes 10485760 | tf_op jit(solution)/shard_map/all_to_all | solution.py:105
  55.9 13.0 %copy-start.10 = (s32[32]{0:T(128)S(1)}, s32[32]{0:T(128)}, u32[]{:S(2)}) copy-start(s32[32]{0:T(128)} %param.8) | copy-start | bytes 388
  56.0 166.8 %collective-permute-start.8 = (f32[5,4,16,1]{3,2,1,0:T(8,128)S(1)}, f32[5,4,16,1]{3,2,1,0:T(8,128)S(1)}, u32[]{:S(2)}, u32[]{:S(2)}) collective-permute-start(f32[5,4,16,1]{3,2,1,0:T(8,128)S(1)} %get-tuple-element.17), channel_id=1, source_target_pairs={{0,8},{8,16},{16,24},{24,32},{32,40},{40,48},{48,56},{56,64},{64,7... | collective-permute-start | bytes 3848 | tf_op jit(solution)/shard_map/ppermute | solution.py:18
  57.7 165.1 %collective-permute-start.9 = (f32[5,4,16,1]{3,2,1,0:T(8,128)S(1)}, f32[5,4,16,1]{3,2,1,0:T(8,128)S(1)}, u32[]{:S(2)}, u32[]{:S(2)}) collective-permute-start(f32[5,4,16,1]{3,2,1,0:T(8,128)S(1)} %get-tuple-element.18), channel_id=1, source_target_pairs={{8,0},{16,8},{24,16},{32,24},{40,32},{48,40},{56,48},{64,56},{72,6... | collective-permute-start | bytes 3848 | tf_op jit(solution)/shard_map/ppermute | solution.py:20
  58.4 192.1 %collective-permute-start.6 = (f32[5,4,1,512]{3,2,1,0:T(1,128)}, f32[5,4,1,512]{3,2,1,0:T(1,128)S(1)}, u32[]{:S(2)}, u32[]{:S(2)}) collective-permute-start(f32[5,4,1,512]{3,2,1,0:T(1,128)} %get-tuple-element.15), channel_id=1, source_target_pairs={{0,1},{1,2},{2,3},{3,4},{4,5},{5,6},{6,7},{8,9},{9,10},{10,11},{11... | collective-permute-start | bytes 122888 | tf_op jit(solution)/shard_map/ppermute | solution.py:18
  64.6 185.9 %collective-permute-start.7 = (f32[5,4,1,512]{3,2,1,0:T(1,128)}, f32[5,4,1,512]{3,2,1,0:T(1,128)S(1)}, u32[]{:S(2)}, u32[]{:S(2)}) collective-permute-start(f32[5,4,1,512]{3,2,1,0:T(1,128)} %get-tuple-element.16), channel_id=1, source_target_pairs={{1,0},{2,1},{3,2},{4,3},{5,4},{6,5},{7,6},{9,8},{10,9},{11,10},{12... | collective-permute-start | bytes 122888 | tf_op jit(solution)/shard_map/ppermute | solution.py:20
  66.9 165.2 %collective-permute-start.3 = (f32[5,8,16,1]{3,2,1,0:T(8,128)}, f32[5,8,16,1]{3,2,1,0:T(8,128)S(1)}, u32[]{:S(2)}, u32[]{:S(2)}) collective-permute-start(f32[5,8,16,1]{3,2,1,0:T(8,128)} %get-tuple-element.11), channel_id=1, source_target_pairs={{0,8},{8,16},{16,24},{24,32},{32,40},{40,48},{48,56},{56,64},{64,7... | collective-permute-start | bytes 7688 | tf_op jit(solution)/shard_map/ppermute | solution.py:18
  222.8 23.2 %collective-permute-start.4 = (f32[5,8,16,1]{3,2,1,0:T(8,128)}, f32[5,8,16,1]{3,2,1,0:T(8,128)S(1)}, u32[]{:S(2)}, u32[]{:S(2)}) collective-permute-start(f32[5,8,16,1]{3,2,1,0:T(8,128)} %get-tuple-element.12), channel_id=1, source_target_pairs={{8,0},{16,8},{24,16},{32,24},{40,32},{48,40},{56,48},{64,56},{72,6... | collective-permute-start | bytes 7688 | tf_op jit(solution)/shard_map/ppermute | solution.py:20
  222.8 29.2 %collective-permute-start.1 = (f32[5,8,1,512]{3,1,2,0:T(8,128)}, f32[5,8,1,512]{3,1,2,0:T(8,128)S(1)}, u32[]{:S(2)}, u32[]{:S(2)}) collective-permute-start(f32[5,8,1,512]{3,1,2,0:T(8,128)} %copy.29), channel_id=1, source_target_pairs={{0,1},{1,2},{2,3},{3,4},{4,5},{5,6},{6,7},{8,9},{9,10},{10,11},{11... | collective-permute-start | bytes 245768 | tf_op jit(solution)/shard_map/ppermute | solution.py:18
  230.8 1.3 copy-start.9
  232.1 19.9 %collective-permute-start.2 = (f32[5,8,1,512]{3,1,2,0:T(8,128)S(1)}, f32[5,8,1,512]{3,1,2,0:T(8,128)S(1)}, u32[]{:S(2)}, u32[]{:S(2)}) collective-permute-start(f32[5,8,1,512]{3,1,2,0:T(8,128)S(1)} %copy-done.9), channel_id=1, source_target_pairs={{1,0},{2,1},{3,2},{4,3},{5,4},{6,5},{7,6},{9,8},{10,9},{11,10},{12... | collective-permute-start | bytes 245768 | tf_op jit(solution)/shard_map/ppermute | solution.py:20
  464.7 13.5 %copy-start.7 = (f32[8,16,512]{2,1,0:T(8,128)S(1)}, f32[8,16,512]{2,1,0:T(8,128)}, u32[]{:S(2)}) copy-start(f32[8,16,512]{2,1,0:T(8,128)} %multiply_bitcast_fusion) | copy-start | bytes 786436
  464.7 18.3 %collective-permute-start.5 = (f32[5,16,512]{2,1,0:T(8,128)}, f32[5,16,512]{2,1,0:T(8,128)}, u32[]{:S(2)}, u32[]{:S(2)}) collective-permute-start(f32[5,16,512]{2,1,0:T(8,128)} %reshape.112), channel_id=1, source_target_pairs={{0,8},{8,16},{16,24},{24,32},{32,40},{40,48},{48,56},{56,64},{64,7... | collective-permute-start | bytes 491528 | tf_op jit(solution)/shard_map/ppermute | solution.py:30
  478.2 1.4 copy-start.3
  478.2 2.0 copy-start.4
  478.5 2.3 copy-start.2
  480.8 3.3 copy-start.8
  484.1 1.1 copy-start.5
  484.1 1.4 copy-start.6
Sparse Core Ops, SparseCore 0:
  14.8 351.4 all-gather.1
